TPU v7x, 512 devices: a whole 4x8x8 slice. The times are simulated.
512 devices in a mesh: row: 16 (over z, core), col: 32 (over x, y).
Axes of the slice: x: 4, y: 8, z: 8, core: 2. Of those that a mesh axis runs over, the one named last changes fastest.
Arguments:
- graph_emb: float32 [16384, 256], P('row', 'col'), may hold values from -40 to 40
- conf_emb: float32 [16384, 256], P('col', 'row'), may hold values from -40 to 40
Outputs:
- grad_graph: float32 [16384, 256], P('row', 'col')
- grad_conf: float32 [16384, 256], P('col', 'row')
- row_potential: float32 [16384], P('row')
- col_potential: float32 [16384], P('col')
All inputs are finite; a program needn't handle non-finite values.
Results may differ from a plain program's by a relative error of at most 0.0003.
Values sent between devices are 32-bit elements; how exact they have to be, the bound alone decides.
No kernel may reach another device: no remote copies, remote signals or barrier semaphores. Data moves between devices by JAX's collectives and lax.ppermute only.
A program may use at most 64 MiB of HBM per device.

v0:
```python
import math
import jax
import jax.numpy as jnp
from jax import lax
from jax.sharding import PartitionSpec as P

ITERS = 3
entropy_weight = 1.0


def across_columns(scores):
    local_max = jnp.max(scores, axis=1)
    peak_value = lax.pmax(local_max, "col")
    exp_total = lax.psum(jnp.sum(jnp.exp(scores - peak_value[:, None]), axis=1), "col")
    return peak_value + jnp.log(exp_total)


def across_rows(scores):
    local_max = jnp.max(scores, axis=0)
    peak_value = lax.pmax(local_max, "row")
    exp_total = lax.psum(jnp.sum(jnp.exp(scores - peak_value[None, :]), axis=0), "row")
    return peak_value + jnp.log(exp_total)


def per_device(graph_emb, conf_emb):
    graph_block = lax.all_gather(graph_emb, "col", axis=1, tiled=True)
    conf_block = lax.all_gather(conf_emb, "row", axis=1, tiled=True)
    batch_size = graph_block.shape[0] * lax.axis_size("row")
    feature_scale = graph_block.shape[1] ** (-0.5)
    cost_tile = (
        -lax.dot_general(
            graph_block,
            conf_block,
            (((1,), (1,)), ((), ())),
            precision=lax.Precision.HIGHEST,
            preferred_element_type=jnp.float32,
        )
        * feature_scale
    )
    log_weight = -math.log(batch_size)
    row_pot = jnp.zeros((graph_block.shape[0],), jnp.float32)
    col_pot = jnp.zeros((conf_block.shape[0],), jnp.float32)
    for sweep_index in range(ITERS):
        row_pot = entropy_weight * (
            log_weight - across_columns((col_pot[None, :] - cost_tile) / entropy_weight)
        )
        col_pot = entropy_weight * (
            log_weight - across_rows((row_pot[:, None] - cost_tile) / entropy_weight)
        )
    transport = jnp.exp((row_pot[:, None] + col_pot[None, :] - cost_tile) / entropy_weight)
    factor = -batch_size * feature_scale
    graph_term = (
        jnp.dot(
            transport,
            conf_block,
            precision=lax.Precision.HIGHEST,
            preferred_element_type=jnp.float32,
        )
        * factor
    )
    conf_term = (
        lax.dot_general(
            transport,
            graph_block,
            (((0,), (0,)), ((), ())),
            precision=lax.Precision.HIGHEST,
            preferred_element_type=jnp.float32,
        )
        * factor
    )
    graph_total = lax.psum(graph_term, "col")
    conf_total = lax.psum(conf_term, "row")
    graph_width = graph_term.shape[1] // lax.axis_size("col")
    conf_width = conf_term.shape[1] // lax.axis_size("row")
    grad_graph = lax.dynamic_slice_in_dim(
        graph_total, lax.axis_index("col") * graph_width, graph_width, 1
    )
    grad_conf = lax.dynamic_slice_in_dim(
        conf_total, lax.axis_index("row") * conf_width, conf_width, 1
    )
    return (grad_graph, grad_conf, row_pot, col_pot)


def solution(mesh):
    return jax.shard_map(
        per_device,
        mesh=mesh,
        in_specs=(P("row", "col"), P("col", "row")),
        out_specs=(P("row", "col"), P("col", "row"), P("row"), P("col")),
        check_vma=False,
    )
```

profile of v0, /device:TPU:64, one launch (start us, length us, event | category | flops | bytes accessed | tf_op | source)
XLA Modules:
  0.0 959.0 jit_solution(13728568763963591692)
XLA Ops:
  7.2 0.0 all-gather.2.cloned.1.call-start
  7.2 0.7 all-gather.2.cloned.1.call-update
  7.9 0.0 all-reduce.5.cloned.1.call-start
  7.9 21.8 %all_gather.7 = f32[512,256]{0,1:T(8,128)S(1)} all-gather(f32[512,16]{0,1:T(8,128)} %param.3), channel_id=1, replica_groups=mesh['row'=16,'col'=32] {'row'}, dimensions={1}, use_global_device_ids=true | all-gather | bytes 557056 | tf_op jit(solution)/shard_map/all_gather | solution.py:27
  29.7 67.0 %all-gather.2.cloned.1.call-done = f32[1024,256]{0,1:T(8,128)} async-done(((f32[1024,8]{0,1:T(8,128)}), f32[1024,256]{0,1:T(8,128)}) %all-gather.2.cloned.1.call-update) | async-done | bytes 1048592 | tf_op jit(solution)/shard_map/all_gather | solution.py:26
  96.7 3.2 subtract_reduce_fusion.5
  99.9 72.0 %pmax.42 = f32[1024]{0:T(1024)S(1)} all-reduce(f32[1024]{0:T(1024)S(1)} %get-tuple-element.4), channel_id=1, replica_groups=mesh['row'=16,'col'=32] {'col'}, use_global_device_ids=true, to_apply=%region_1.0 | all-reduce | flops 1024 | bytes 8192 | tf_op jit(solution)/shard_map/pmax | solution.py:13
  172.0 0.5 exponential_reduce_fusion.5
  172.5 69.6 %psum.56 = f32[1024]{0:T(1024)S(1)} all-reduce(f32[1024]{0:T(1024)S(1)} %exponential_reduce_fusion.5), channel_id=1, replica_groups=mesh['row'=16,'col'=32] {'col'}, use_global_device_ids=true, to_apply=%region_3.0 | all-reduce | flops 1024 | bytes 8192 | tf_op jit(solution)/shard_map/psum | solution.py:14
  242.2 0.2 subtract_reduce_fusion.4
  242.4 21.1 %pmax.43 = f32[512]{0:T(512)S(1)} all-reduce(f32[512]{0:T(512)S(1)} %subtract_reduce_fusion.4), channel_id=1, replica_groups=mesh['row'=16,'col'=32] {'row'}, use_global_device_ids=true, to_apply=%region_5.0 | all-reduce | flops 512 | bytes 4096 | tf_op jit(solution)/shard_map/pmax | solution.py:20
  263.5 0.4 exponential_reduce_fusion.4
  263.9 23.9 %psum.57 = f32[512]{0:T(512)S(1)} all-reduce(f32[512]{0:T(512)S(1)} %exponential_reduce_fusion.4), channel_id=1, replica_groups=mesh['row'=16,'col'=32] {'row'}, use_global_device_ids=true, to_apply=%region_7.0 | all-reduce | flops 512 | bytes 4096 | tf_op jit(solution)/shard_map/psum | solution.py:21
  287.8 0.2 subtract_reduce_fusion.3
  288.0 71.7 %pmax.44 = f32[1024]{0:T(1024)S(1)} all-reduce(f32[1024]{0:T(1024)S(1)} %subtract_reduce_fusion.3), channel_id=1, replica_groups=mesh['row'=16,'col'=32] {'col'}, use_global_device_ids=true, to_apply=%region_9.0 | all-reduce | flops 1024 | bytes 8192 | tf_op jit(solution)/shard_map/pmax | solution.py:13
  359.7 0.6 exponential_reduce_fusion.3
  360.3 69.6 %psum.58 = f32[1024]{0:T(1024)S(1)} all-reduce(f32[1024]{0:T(1024)S(1)} %exponential_reduce_fusion.3), channel_id=1, replica_groups=mesh['row'=16,'col'=32] {'col'}, use_global_device_ids=true, to_apply=%region_11.0 | all-reduce | flops 1024 | bytes 8192 | tf_op jit(solution)/shard_map/psum | solution.py:14
  429.9 0.2 subtract_reduce_fusion.2
  430.1 23.5 %pmax.45 = f32[512]{0:T(512)S(1)} all-reduce(f32[512]{0:T(512)S(1)} %subtract_reduce_fusion.2), channel_id=1, replica_groups=mesh['row'=16,'col'=32] {'row'}, use_global_device_ids=true, to_apply=%region_13.0 | all-reduce | flops 512 | bytes 4096 | tf_op jit(solution)/shard_map/pmax | solution.py:20
  453.7 0.4 exponential_reduce_fusion.2
  454.1 23.5 %psum.59 = f32[512]{0:T(512)S(1)} all-reduce(f32[512]{0:T(512)S(1)} %exponential_reduce_fusion.2), channel_id=1, replica_groups=mesh['row'=16,'col'=32] {'row'}, use_global_device_ids=true, to_apply=%region_15.0 | all-reduce | flops 512 | bytes 4096 | tf_op jit(solution)/shard_map/psum | solution.py:21
  477.7 0.2 subtract_reduce_fusion.1
  477.9 71.6 %pmax.46 = f32[1024]{0:T(1024)S(1)} all-reduce(f32[1024]{0:T(1024)S(1)} %subtract_reduce_fusion.1), channel_id=1, replica_groups=mesh['row'=16,'col'=32] {'col'}, use_global_device_ids=true, to_apply=%region_17.0 | all-reduce | flops 1024 | bytes 8192 | tf_op jit(solution)/shard_map/pmax | solution.py:13
  549.5 0.6 exponential_reduce_fusion.1
  550.1 69.6 %psum.60 = f32[1024]{0:T(1024)S(1)} all-reduce(f32[1024]{0:T(1024)S(1)} %exponential_reduce_fusion.1), channel_id=1, replica_groups=mesh['row'=16,'col'=32] {'col'}, use_global_device_ids=true, to_apply=%region_19.0 | all-reduce | flops 1024 | bytes 8192 | tf_op jit(solution)/shard_map/psum | solution.py:14
  619.8 0.0 copy-start
  619.8 0.2 subtract_reduce_fusion
  620.0 23.5 %pmax.47 = f32[512]{0:T(512)S(1)} all-reduce(f32[512]{0:T(512)S(1)} %subtract_reduce_fusion), channel_id=1, replica_groups=mesh['row'=16,'col'=32] {'row'}, use_global_device_ids=true, to_apply=%region_21.0 | all-reduce | flops 512 | bytes 4096 | tf_op jit(solution)/shard_map/pmax | solution.py:20
  643.5 0.4 exponential_reduce_fusion
  644.0 23.5 %psum.61 = f32[512]{0:T(512)S(1)} all-reduce(f32[512]{0:T(512)S(1)} %exponential_reduce_fusion), channel_id=1, replica_groups=mesh['row'=16,'col'=32] {'row'}, use_global_device_ids=true, to_apply=%region_23.0 | all-reduce | flops 512 | bytes 4096 | tf_op jit(solution)/shard_map/psum | solution.py:21
  667.5 0.0 copy-start.1
  667.5 4.4 fusion.3
  671.9 0.0 all-reduce.5.cloned.1.call-update
  672.0 0.2 all-reduce.3.cloned.1.call-start
  672.2 0.0 copy-done
  672.2 0.0 copy-done.1
  672.2 3.4 fusion.2
  675.6 0.0 all-reduce.3.cloned.1.call-update
  675.6 108.3 %all-reduce.5.cloned.1.call-done = f32[512,256]{0,1:T(8,128)} async-done(((f32[512,256]{0,1:T(8,128)}), f32[512,256]{0,1:T(8,128)}) %all-reduce.5.cloned.1.call-update) | async-done | bytes 524304 | tf_op jit(solution)/shard_map/psum | solution.py:72
  783.9 1.4 constant_dynamic-slice_fusion
  785.3 165.8 %all-reduce.3.cloned.1.call-done = f32[1024,256]{0,1:T(8,128)} async-done(((f32[1024,256]{0,1:T(8,128)}), f32[1024,256]{0,1:T(8,128)}) %all-reduce.3.cloned.1.call-update) | async-done | bytes 1048592 | tf_op jit(solution)/shard_map/psum | solution.py:71
  951.1 1.4 constant_dynamic-slice_fusion.1
  (6 shorter events, 0.1 us)
Async XLA Ops:
  7.2 89.5 %all-gather.2.cloned.1.call-start = ((), (), s32[]{:S(2)}) async-start(), calls=%async_computation | async-start | bytes 1081344 | tf_op jit(solution)/shard_map/all_gather | solution.py:26
  7.9 776.0 %all-reduce.5.cloned.1.call-start = ((), (), s32[]{:S(2)}) async-start(), calls=%async_computation.2 | async-start | bytes 1048576 | tf_op jit(solution)/shard_map/psum | solution.py:72
  619.8 52.4 %copy-start = (f32[1024]{0:T(1024)}, f32[1024]{0:T(1024)S(1)}, u32[]{:S(2)}) copy-start(f32[1024]{0:T(1024)S(1)} %add_subtract_fusion) | copy-start | bytes 12292
  667.5 4.7 copy-start.1
  672.0 279.2 %all-reduce.3.cloned.1.call-start = ((), (), s32[]{:S(2)}) async-start(), calls=%async_computation.1 | async-start | bytes 2097152 | tf_op jit(solution)/shard_map/psum | solution.py:71
Sparse Core Ops, SparseCore 0:
  11.1 85.4 all-gather.1
  672.1 111.8 all-reduce.4
  787.4 163.6 all-reduce.2
where the time goes:
time: 960 us; the launch traced here: 959 us
  blocking collectives  585 us (61%)
  waiting for transfers between devices  342 us (36%)
  between operations  13.8 us (1%)
  matrix products  11 us (1%)
    pmax x3, blocking collectives, across_columns(): peak_value = lax.pmax(local_max, 'col')  215 us
    psum x3, blocking collectives, across_columns(): lax.psum(jnp.sum(jnp.exp(scores - peak_value[:, None]), axis=1), 'col')  209 us
    psum x1, waiting for transfers between devices, per_device(): graph_total = lax.psum(graph_term, 'col')  166 us
    psum x1, waiting for transfers between devices, per_device(): conf_total = lax.psum(conf_term, 'row')  108 us
    psum x3, blocking collectives, across_rows(): lax.psum(jnp.sum(jnp.exp(scores - peak_value[None, :]), axis=0), 'row')  71 us
    pmax x3, blocking collectives, across_rows(): peak_value = lax.pmax(local_max, 'row')  68.2 us
    all_gather x1, waiting for transfers between devices, per_device(): graph_block = lax.all_gather(graph_emb, 'col', axis=1, tiled=True)  67 us
    all_gather x1, blocking collectives, per_device(): conf_block = lax.all_gather(conf_emb, 'row', axis=1, tiled=True)  21.8 us
  transfers between devices with their start and end apart: 3, of which 3 were waited for; matrix products, arithmetic and copies ran while one was open for 0% of the time, Pallas kernels for 0%

commit v1 on v0

--- a/solution.py
+++ b/solution.py
@@ -23,7 +23,9 @@
 
 
 def per_device(graph_emb, conf_emb):
-    graph_block = lax.all_gather(graph_emb, "col", axis=1, tiled=True)
+    graph_block = jnp.concatenate(
+        lax.all_to_all(jnp.stack([graph_emb] * lax.axis_size("col")), "col", 0, 0), axis=1
+    )
     conf_block = lax.all_gather(conf_emb, "row", axis=1, tiled=True)
     batch_size = graph_block.shape[0] * lax.axis_size("row")
     feature_scale = graph_block.shape[1] ** (-0.5)

time: 960 us -> 913 us (0.951)
  waiting for transfers between devices: 342 us -> 279 us
  starting transfers between devices: 0.3 us -> 10.3 us
    all_gather x1 -> x0, waiting for transfers between devices: 67 us -> none  [per_device(): graph_block = lax.all_gather(graph_emb, 'col', axis=1, tiled=True)]
    all_to_all x0 -> x1, starting transfers between devices: none -> 10.1 us  [per_device(): lax.all_to_all(jnp.stack([graph_emb] * lax.axis_size('col')), 'col', 0, 0)]
  transfers between devices with their start and end apart: 3 -> 3, of which waited for: 3 -> 3; matrix products, arithmetic and copies ran while one was open for 0% -> 1% of each run, Pallas kernels for 0% -> 0%
where the time goes in v1:
time: 913 us; the launch traced here: 912 us
  blocking collectives  589 us (65%)
  waiting for transfers between devices  279 us (31%)
  between operations  14.1 us (2%)
  matrix products  11 us (1%)
  starting transfers between devices  10.3 us (1%)
    pmax x3, blocking collectives, across_columns(): peak_value = lax.pmax(local_max, 'col')  215 us
    psum x3, blocking collectives, across_columns(): lax.psum(jnp.sum(jnp.exp(scores - peak_value[:, None]), axis=1), 'col')  209 us
    psum x1, waiting for transfers between devices, per_device(): graph_total = lax.psum(graph_term, 'col')  166 us
    psum x1, waiting for transfers between devices, per_device(): conf_total = lax.psum(conf_term, 'row')  106 us
    pmax x3, blocking collectives, across_rows(): peak_value = lax.pmax(local_max, 'row')  72.5 us
    psum x3, blocking collectives, across_rows(): lax.psum(jnp.sum(jnp.exp(scores - peak_value[None, :]), axis=0), 'row')  71 us
    all_gather x1, blocking collectives, per_device(): conf_block = lax.all_gather(conf_emb, 'row', axis=1, tiled=True)  21.6 us
  transfers between devices with their start and end apart: 3, of which 3 were waited for; matrix products, arithmetic and copies ran while one was open for 1% of the time, Pallas kernels for 0%

profile of v1, /device:TPU:64, one launch (start us, length us, event | category | flops | bytes accessed | tf_op | source)
XLA Modules:
  0.0 912.5 jit_solution(6976317515702388879)
XLA Ops:
  7.2 0.0 copy-start.1
  7.2 1.9 stack.2
  9.1 10.1 %all-to-all-start = ((f32[32,1024,8]{1,2,0:T(8,128)}), f32[32,1024,8]{1,2,0:T(8,128)}, u32[]{:S(2)}, u32[]{:S(2)}) async-start(f32[32,1024,8]{1,2,0:T(8,128)} %stack.2), calls=%async_computation | async-start | bytes 2097152 | tf_op jit(solution)/shard_map/all_to_all | solution.py:27
  19.2 0.0 all-reduce.5.cloned.1.call-start
  19.2 0.0 copy-done.1
  19.2 21.6 %all_gather.3 = f32[512,256]{0,1:T(8,128)S(1)} all-gather(f32[512,16]{0,1:T(8,128)S(1)} %copy-done.1), channel_id=1, replica_groups=mesh['row'=16,'col'=32] {'row'}, dimensions={1}, use_global_device_ids=true | all-gather | bytes 557056 | tf_op jit(solution)/shard_map/all_gather | solution.py:29
  40.8 7.0 all-to-all-done
  47.8 3.2 subtract_reduce_fusion.5
  51.0 72.0 %pmax.42 = f32[1024]{0:T(1024)S(1)} all-reduce(f32[1024]{0:T(1024)S(1)} %get-tuple-element.4), channel_id=1, replica_groups=mesh['row'=16,'col'=32] {'col'}, use_global_device_ids=true, to_apply=%region_1.0 | all-reduce | flops 1024 | bytes 8192 | tf_op jit(solution)/shard_map/pmax | solution.py:13
  123.0 0.5 exponential_reduce_fusion.5
  123.5 69.6 %psum.56 = f32[1024]{0:T(1024)S(1)} all-reduce(f32[1024]{0:T(1024)S(1)} %exponential_reduce_fusion.5), channel_id=1, replica_groups=mesh['row'=16,'col'=32] {'col'}, use_global_device_ids=true, to_apply=%region_3.0 | all-reduce | flops 1024 | bytes 8192 | tf_op jit(solution)/shard_map/psum | solution.py:14
  193.2 0.2 subtract_reduce_fusion.4
  193.4 25.4 %pmax.43 = f32[512]{0:T(512)S(1)} all-reduce(f32[512]{0:T(512)S(1)} %subtract_reduce_fusion.4), channel_id=1, replica_groups=mesh['row'=16,'col'=32] {'row'}, use_global_device_ids=true, to_apply=%region_5.0 | all-reduce | flops 512 | bytes 4096 | tf_op jit(solution)/shard_map/pmax | solution.py:20
  218.8 0.4 exponential_reduce_fusion.4
  219.3 23.9 %psum.57 = f32[512]{0:T(512)S(1)} all-reduce(f32[512]{0:T(512)S(1)} %exponential_reduce_fusion.4), channel_id=1, replica_groups=mesh['row'=16,'col'=32] {'row'}, use_global_device_ids=true, to_apply=%region_7.0 | all-reduce | flops 512 | bytes 4096 | tf_op jit(solution)/shard_map/psum | solution.py:21
  243.2 0.2 subtract_reduce_fusion.3
  243.4 71.7 %pmax.44 = f32[1024]{0:T(1024)S(1)} all-reduce(f32[1024]{0:T(1024)S(1)} %subtract_reduce_fusion.3), channel_id=1, replica_groups=mesh['row'=16,'col'=32] {'col'}, use_global_device_ids=true, to_apply=%region_9.0 | all-reduce | flops 1024 | bytes 8192 | tf_op jit(solution)/shard_map/pmax | solution.py:13
  315.1 0.6 exponential_reduce_fusion.3
  315.6 69.6 %psum.58 = f32[1024]{0:T(1024)S(1)} all-reduce(f32[1024]{0:T(1024)S(1)} %exponential_reduce_fusion.3), channel_id=1, replica_groups=mesh['row'=16,'col'=32] {'col'}, use_global_device_ids=true, to_apply=%region_11.0 | all-reduce | flops 1024 | bytes 8192 | tf_op jit(solution)/shard_map/psum | solution.py:14
  385.3 0.2 subtract_reduce_fusion.2
  385.5 23.5 %pmax.45 = f32[512]{0:T(512)S(1)} all-reduce(f32[512]{0:T(512)S(1)} %subtract_reduce_fusion.2), channel_id=1, replica_groups=mesh['row'=16,'col'=32] {'row'}, use_global_device_ids=true, to_apply=%region_13.0 | all-reduce | flops 512 | bytes 4096 | tf_op jit(solution)/shard_map/pmax | solution.py:20
  409.0 0.4 exponential_reduce_fusion.2
  409.5 23.5 %psum.59 = f32[512]{0:T(512)S(1)} all-reduce(f32[512]{0:T(512)S(1)} %exponential_reduce_fusion.2), channel_id=1, replica_groups=mesh['row'=16,'col'=32] {'row'}, use_global_device_ids=true, to_apply=%region_15.0 | all-reduce | flops 512 | bytes 4096 | tf_op jit(solution)/shard_map/psum | solution.py:21
  433.0 0.2 subtract_reduce_fusion.1
  433.3 71.6 %pmax.46 = f32[1024]{0:T(1024)S(1)} all-reduce(f32[1024]{0:T(1024)S(1)} %subtract_reduce_fusion.1), channel_id=1, replica_groups=mesh['row'=16,'col'=32] {'col'}, use_global_device_ids=true, to_apply=%region_17.0 | all-reduce | flops 1024 | bytes 8192 | tf_op jit(solution)/shard_map/pmax | solution.py:13
  504.9 0.6 exponential_reduce_fusion.1
  505.4 69.6 %psum.60 = f32[1024]{0:T(1024)S(1)} all-reduce(f32[1024]{0:T(1024)S(1)} %exponential_reduce_fusion.1), channel_id=1, replica_groups=mesh['row'=16,'col'=32] {'col'}, use_global_device_ids=true, to_apply=%region_19.0 | all-reduce | flops 1024 | bytes 8192 | tf_op jit(solution)/shard_map/psum | solution.py:14
  575.1 0.0 copy-start
  575.1 0.2 subtract_reduce_fusion
  575.3 23.5 %pmax.47 = f32[512]{0:T(512)S(1)} all-reduce(f32[512]{0:T(512)S(1)} %subtract_reduce_fusion), channel_id=1, replica_groups=mesh['row'=16,'col'=32] {'row'}, use_global_device_ids=true, to_apply=%region_21.0 | all-reduce | flops 512 | bytes 4096 | tf_op jit(solution)/shard_map/pmax | solution.py:20
  598.9 0.4 exponential_reduce_fusion
  599.3 23.5 %psum.61 = f32[512]{0:T(512)S(1)} all-reduce(f32[512]{0:T(512)S(1)} %exponential_reduce_fusion), channel_id=1, replica_groups=mesh['row'=16,'col'=32] {'row'}, use_global_device_ids=true, to_apply=%region_23.0 | all-reduce | flops 512 | bytes 4096 | tf_op jit(solution)/shard_map/psum | solution.py:21
  622.9 0.0 copy-start.2
  622.9 4.4 fusion.3
  627.3 0.0 all-reduce.5.cloned.1.call-update
  627.3 0.2 all-reduce.3.cloned.1.call-start
  627.5 0.0 copy-done
  627.5 0.0 copy-done.2
  627.6 3.4 fusion.2
  630.9 0.0 all-reduce.3.cloned.1.call-update
  630.9 106.2 %all-reduce.5.cloned.1.call-done = f32[512,256]{0,1:T(8,128)} async-done(((f32[512,256]{0,1:T(8,128)}), f32[512,256]{0,1:T(8,128)}) %all-reduce.5.cloned.1.call-update) | async-done | bytes 524304 | tf_op jit(solution)/shard_map/psum | solution.py:74
  737.1 1.4 constant_dynamic-slice_fusion
  738.5 165.8 %all-reduce.3.cloned.1.call-done = f32[1024,256]{0,1:T(8,128)} async-done(((f32[1024,256]{0,1:T(8,128)}), f32[1024,256]{0,1:T(8,128)}) %all-reduce.3.cloned.1.call-update) | async-done | bytes 1048592 | tf_op jit(solution)/shard_map/psum | solution.py:73
  904.3 1.4 constant_dynamic-slice_fusion.1
  (6 shorter events, 0.1 us)
Async XLA Ops:
  7.2 12.1 %copy-start.1 = (f32[512,16]{0,1:T(8,128)S(1)}, f32[512,16]{0,1:T(8,128)}, u32[]{:S(2)}) copy-start(f32[512,16]{0,1:T(8,128)} %param.3) | copy-start | bytes 98308
  9.1 38.7 %all-to-all-start = ((f32[32,1024,8]{1,2,0:T(8,128)}), f32[32,1024,8]{1,2,0:T(8,128)}, u32[]{:S(2)}, u32[]{:S(2)}) async-start(f32[32,1024,8]{1,2,0:T(8,128)} %stack.2), calls=%async_computation | async-start | bytes 2097152 | tf_op jit(solution)/shard_map/all_to_all | solution.py:27
  19.2 717.9 %all-reduce.5.cloned.1.call-start = ((), (), s32[]{:S(2)}) async-start(), calls=%async_computation.2 | async-start | bytes 1048576 | tf_op jit(solution)/shard_map/psum | solution.py:74
  575.1 52.4 %copy-start = (f32[1024]{0:T(1024)}, f32[1024]{0:T(1024)S(1)}, u32[]{:S(2)}) copy-start(f32[1024]{0:T(1024)S(1)} %add_subtract_fusion) | copy-start | bytes 12292
  622.9 4.7 copy-start.2
  627.3 277.0 %all-reduce.3.cloned.1.call-start = ((), (), s32[]{:S(2)}) async-start(), calls=%async_computation.1 | async-start | bytes 2097152 | tf_op jit(solution)/shard_map/psum | solution.py:73
Sparse Core Ops, SparseCore 0:
  627.4 109.6 all-reduce.4
  740.5 163.6 all-reduce.2
